TPU v7x, 512 devices: a whole 4x8x8 slice. The times are simulated.
512 devices in a mesh: seq: 128 (over x, y_lo, z, core), head: 4 (over y_hi).
Axes of the slice: x: 4, y: 8 (y_hi: 4, y_lo: 2; y = y_hi * 2 + y_lo), z: 8, core: 2. Of those that a mesh axis runs over, the one named last changes fastest.
Arguments:
- query_rows: bfloat16 [65536, 2048], P(('seq', 'head')), may hold values from -48 to 48
- key_rows: bfloat16 [65536, 1024], P(('seq', 'head')), may hold values from -16 to 16
- saved_value_rows: bfloat16 [65536, 1024], P(('seq', 'head')), may hold values from -6 to 6
- out_grad: bfloat16 [65536, 2048], P(('seq', 'head')), may hold values from -6 to 6
Outputs:
- query_grad: bfloat16 [65536, 2048], P(('seq', 'head'))
- key_grad: bfloat16 [65536, 1024], P(('seq', 'head'))
- value_grad: bfloat16 [65536, 1024], P(('seq', 'head'))
All inputs are finite; a program needn't handle non-finite values.
Results may differ from a plain program's by a relative error of at most 0.013.
Values may be sent and summed in bfloat16 or wider, within the bound.
A program may use at most 64 MiB of HBM per device.

v0:
```python
import jax
import jax.numpy as jnp
from jax import lax
from jax.sharding import PartitionSpec as P

HEAD_SIZE = 128
W = 1024


score_scale = 168.0 ** (-0.5)
masked_value = -1e30
contract_last = (((1,), (1,)), ((), ()))
contract_first = (((0,), (0,)), ((), ()))


def shifted(value, axis, steps):
    count = lax.axis_size(axis)
    first, last = (max(0, -steps), min(count, count - steps))
    return lax.ppermute(value, axis, [(source, source + steps) for source in range(first, last)])


def on_device(query_rows, key_rows, saved_value_rows, out_grad):
    queries, keys_mine, values_mine, grads_out = (
        lax.all_to_all(query_rows, "head", split_axis=1, concat_axis=0, tiled=True),
        lax.all_to_all(key_rows, "head", split_axis=1, concat_axis=0, tiled=True),
        lax.all_to_all(saved_value_rows, "head", split_axis=1, concat_axis=0, tiled=True),
        lax.all_to_all(out_grad, "head", split_axis=1, concat_axis=0, tiled=True),
    )
    shard_rows = queries.shape[0]
    head_count = queries.shape[1] // HEAD_SIZE
    group_count = keys_mine.shape[1] // HEAD_SIZE
    keys_near, values_near = shifted((keys_mine, values_mine), "seq", 1)
    keys_far, values_far = shifted((keys_mine, values_mine), "seq", 2)
    keys_all = jnp.concatenate([keys_far, keys_near, keys_mine], 0)
    values_all = jnp.concatenate([values_far, values_near, values_mine], 0)
    anchor = lax.axis_index("seq") * shard_rows
    query_pos = anchor + jnp.arange(shard_rows, dtype=jnp.int32)
    key_pos = anchor - 2 * shard_rows + jnp.arange(3 * shard_rows, dtype=jnp.int32)
    distance = query_pos[:, None] - key_pos[None, :]
    visible = (distance >= 0) & (distance < W) & (key_pos[None, :] >= 0)
    zero_block = jnp.zeros((3 * shard_rows, HEAD_SIZE), jnp.float32)
    key_parts = [zero_block] * group_count
    value_parts = [zero_block] * group_count
    query_parts = []
    for q_head in range(head_count):
        kv_group = q_head // 2
        query_head = queries[:, q_head * HEAD_SIZE : (q_head + 1) * HEAD_SIZE]
        grad_head = grads_out[:, q_head * HEAD_SIZE : (q_head + 1) * HEAD_SIZE]
        key_head = keys_all[:, kv_group * HEAD_SIZE : (kv_group + 1) * HEAD_SIZE]
        value_head = values_all[:, kv_group * HEAD_SIZE : (kv_group + 1) * HEAD_SIZE]
        scores = (
            lax.dot_general(query_head, key_head, contract_last, preferred_element_type=jnp.float32)
            * score_scale
        )
        scores = jnp.where(visible, scores, masked_value)
        row_max = jnp.max(scores, axis=1, keepdims=True)
        weights = jnp.exp(scores - row_max)
        attention = weights / jnp.sum(weights, axis=1, keepdims=True)
        attention_low = attention.astype(jnp.bfloat16)
        prob_grad = lax.dot_general(
            grad_head, value_head, contract_last, preferred_element_type=jnp.float32
        )
        row_delta = jnp.sum(attention * prob_grad, axis=1, keepdims=True)
        score_grad = (score_scale * attention * (prob_grad - row_delta)).astype(jnp.bfloat16)
        query_parts.append(
            jnp.dot(score_grad, key_head, preferred_element_type=jnp.float32).astype(jnp.bfloat16)
        )
        key_parts[kv_group] = key_parts[kv_group] + lax.dot_general(
            score_grad, query_head, contract_first, preferred_element_type=jnp.float32
        )
        value_parts[kv_group] = value_parts[kv_group] + lax.dot_general(
            attention_low, grad_head, contract_first, preferred_element_type=jnp.float32
        )
    query_grad = jnp.concatenate(query_parts, 1)
    key_sums = jnp.concatenate(key_parts, 1)
    value_sums = jnp.concatenate(value_parts, 1)
    key_own = key_sums[2 * shard_rows :]
    value_own = value_sums[2 * shard_rows :]
    key_before = key_sums[shard_rows : 2 * shard_rows]
    value_before = value_sums[shard_rows : 2 * shard_rows]
    key_earlier = key_sums[:shard_rows]
    value_earlier = value_sums[:shard_rows]
    back_near = (
        shifted(key_before.astype(jnp.bfloat16), "seq", -1).astype(key_before.dtype),
        shifted(value_before.astype(jnp.bfloat16), "seq", -1).astype(value_before.dtype),
    )
    back_far = (
        shifted(key_earlier.astype(jnp.bfloat16), "seq", -2).astype(key_earlier.dtype),
        shifted(value_earlier.astype(jnp.bfloat16), "seq", -2).astype(value_earlier.dtype),
    )
    key_total = key_own + back_near[0] + back_far[0]
    value_total = value_own + back_near[1] + back_far[1]
    key_grad = key_total.astype(jnp.bfloat16)
    value_grad = value_total.astype(jnp.bfloat16)
    return (
        lax.all_to_all(query_grad, "head", split_axis=0, concat_axis=1, tiled=True),
        lax.all_to_all(key_grad, "head", split_axis=0, concat_axis=1, tiled=True),
        lax.all_to_all(value_grad, "head", split_axis=0, concat_axis=1, tiled=True),
    )


def solution(mesh):
    in_specs = (
        P(("seq", "head"), None),
        P(("seq", "head"), None),
        P(("seq", "head"), None),
        P(("seq", "head"), None),
    )
    out_specs = (P(("seq", "head"), None), P(("seq", "head"), None), P(("seq", "head"), None))
    return jax.shard_map(
        on_device, mesh=mesh, in_specs=in_specs, out_specs=out_specs, check_vma=False
    )
```

profile of v0, /device:TPU:136, one launch (start us, length us, event | category | flops | bytes accessed | tf_op | source)
XLA Modules:
  0.0 169.4 jit_solution(11627586745176453231)
XLA Ops:
  0.6 1.8 %copy.28 = bf16[128,1024]{0,1:T(8,128)(2,1)} copy(bf16[128,1024]{1,0:T(8,128)(2,1)} %param.6) | data formatting | bytes 524288 | tf_op args[2]
  2.5 6.2 %all-to-all-start.2 = ((bf16[128,4,256]{0,2,1:T(8,128)(2,1)}), bf16[128,4,256]{0,2,1:T(8,128)(2,1)S(1)}, u32[]{:S(2)}, u32[]{:S(2)}) async-start(bf16[128,4,256]{0,2,1:T(8,128)(2,1)} %bitcast.7), calls=%async_computation.2 | async-start | bytes 524288 | tf_op jit(solution)/shard_map/all_to_all | solution.py:26
  10.5 8.2 %all-to-all-done.2 = bf16[128,4,256]{0,2,1:T(8,128)(2,1)S(1)} async-done(((bf16[128,4,256]{0,2,1:T(8,128)(2,1)}), bf16[128,4,256]{0,2,1:T(8,128)(2,1)S(1)}, u32[]{:S(2)}, u32[]{:S(2)}) %all-to-all-start.2) | async-done | bytes 262176 | tf_op jit(solution)/shard_map/all_to_all | solution.py:26
  18.7 3.9 %all-to-all-start = ((bf16[128,4,256]{0,2,1:T(8,128)(2,1)}), bf16[128,4,256]{0,2,1:T(8,128)(2,1)S(1)}, u32[]{:S(2)}, u32[]{:S(2)}) async-start(bf16[128,4,256]{0,2,1:T(8,128)(2,1)} %bitcast), calls=%async_computation | async-start | bytes 524288 | tf_op jit(solution)/shard_map/all_to_all | solution.py:25
  22.5 2.0 %copy.26 = bf16[128,2048]{0,1:T(8,128)(2,1)} copy(bf16[128,2048]{1,0:T(8,128)(2,1)} %param.4) | data formatting | bytes 1048576 | tf_op args[0]
  24.7 1.9 %collective-permute-start.3 = (bf16[512,256]{1,0:T(8,128)(2,1)S(1)}, bf16[512,256]{1,0:T(8,128)(2,1)S(1)}, u32[]{:S(2)}, u32[]{:S(2)}) collective-permute-start(bf16[512,256]{1,0:T(8,128)(2,1)S(1)} %bitcast.82), channel_id=1, source_target_pairs={{0,4},{4,8},{8,12},{12,16},{16,20},{20,24},{24,28},{28,32},{32,36}... | collective-permute-start | bytes 786440 | tf_op jit(solution)/shard_map/ppermute | solution.py:19
  26.6 4.3 %collective-permute-start.2 = (bf16[512,256]{1,0:T(8,128)(2,1)S(1)}, bf16[512,256]{1,0:T(8,128)(2,1)S(1)}, u32[]{:S(2)}, u32[]{:S(2)}) collective-permute-start(bf16[512,256]{1,0:T(8,128)(2,1)S(1)} %bitcast.83), channel_id=1, source_target_pairs={{0,8},{4,12},{8,16},{12,20},{16,24},{20,28},{24,32},{28,36},{32,40... | collective-permute-start | bytes 786440 | tf_op jit(solution)/shard_map/ppermute | solution.py:19
  32.7 5.4 %all-to-all-start.1 = ((bf16[128,4,512]{0,2,1:T(8,128)(2,1)}), bf16[128,4,512]{0,2,1:T(8,128)(2,1)S(1)}, u32[]{:S(2)}, u32[]{:S(2)}) async-start(bf16[128,4,512]{0,2,1:T(8,128)(2,1)} %bitcast.3), calls=%async_computation.1 | async-start | bytes 1048576 | tf_op jit(solution)/shard_map/all_to_all | solution.py:24
  38.3 5.0 %collective-permute-start.1 = (bf16[512,256]{1,0:T(8,128)(2,1)S(1)}, bf16[512,256]{1,0:T(8,128)(2,1)S(1)}, u32[]{:S(2)}, u32[]{:S(2)}) collective-permute-start(bf16[512,256]{1,0:T(8,128)(2,1)S(1)} %bitcast.85), channel_id=1, source_target_pairs={{0,4},{4,8},{8,12},{12,16},{16,20},{20,24},{24,28},{28,32},{32,36}... | collective-permute-start | bytes 786440 | tf_op jit(solution)/shard_map/ppermute | solution.py:19
  43.4 3.4 %collective-permute-start = (bf16[512,256]{1,0:T(8,128)(2,1)S(1)}, bf16[512,256]{1,0:T(8,128)(2,1)S(1)}, u32[]{:S(2)}, u32[]{:S(2)}) collective-permute-start(bf16[512,256]{1,0:T(8,128)(2,1)S(1)} %bitcast.86), channel_id=1, source_target_pairs={{0,8},{4,12},{8,16},{12,20},{16,24},{20,28},{24,32},{28,36},{32,40... | collective-permute-start | bytes 786440 | tf_op jit(solution)/shard_map/ppermute | solution.py:19
  48.7 5.3 %collective-permute-done = bf16[512,256]{1,0:T(8,128)(2,1)S(1)} collective-permute-done((bf16[512,256]{1,0:T(8,128)(2,1)S(1)}, bf16[512,256]{1,0:T(8,128)(2,1)S(1)}, u32[]{:S(2)}, u32[]{:S(2)}) %collective-permute-start) | collective-permute-done | bytes 262176 | tf_op jit(solution)/shard_map/ppermute | solution.py:19
  54.1 7.2 %all-to-all-start.3 = ((bf16[128,4,512]{0,2,1:T(8,128)(2,1)}), bf16[128,4,512]{0,2,1:T(8,128)(2,1)}, u32[]{:S(2)}, u32[]{:S(2)}) async-start(bf16[128,4,512]{0,2,1:T(8,128)(2,1)} %bitcast.10), calls=%async_computation.3 | async-start | bytes 1048576 | tf_op jit(solution)/shard_map/all_to_all | solution.py:27
  61.5 3.1 %fusion.72 = (f32[512]{0:T(512)S(1)}, f32[512,1536]{0,1:T(8,128)}) fusion(bf16[512,512]{1,0:T(8,128)(2,1)S(1)} %bitcast.68, bf16[1536,256]{1,0:T(8,128)(2,1)S(1)} %pad_maximum_fusion.2, pred[1536]{0:T(1024)(128)(4,1)S(1)} %broadcast_compare_fusion, s32[1536]{0:T(1024)S(1)} %iota_add_fusion, s32[512]{0:T(512)S(1)} %iota_add_fusion.1), kind=kOutput, calls=%fused_computation.113 | convolution fusion | flops 207617536 | bytes 3684352 | tf_op jit(solution)/shard_map/dot_general | solution.py:52
  64.6 3.1 %fusion.73 = (f32[512]{0:T(512)S(1)}, f32[512,1536]{0,1:T(8,128)}) fusion(bf16[512,512]{1,0:T(8,128)(2,1)S(1)} %bitcast.69, bf16[1536,256]{1,0:T(8,128)(2,1)S(1)} %pad_maximum_fusion.2, pred[1536]{0:T(1024)(128)(4,1)S(1)} %broadcast_compare_fusion, s32[1536]{0:T(1024)S(1)} %iota_add_fusion, s32[512]{0:T(512)S(1)} %iota_add_fusion.1), kind=kOutput, calls=%fused_computation.114 | convolution fusion | flops 207617536 | bytes 3684352 | tf_op jit(solution)/shard_map/dot_general | solution.py:52
  67.7 2.6 %fusion.74 = (f32[512]{0:T(512)S(1)}, f32[512,1536]{0,1:T(8,128)S(1)}) fusion(bf16[512,512]{1,0:T(8,128)(2,1)} %bitcast.70, bf16[1536,256]{1,0:T(8,128)(2,1)} %copy-done.10, pred[1536]{0:T(1024)(128)(4,1)S(1)} %broadcast_compare_fusion, s32[1536]{0:T(1024)S(1)} %iota_add_fusion, s32[512]{0:T(512)S(1)} %iota_add_fusion.1), kind=kOutput, calls=%fused_computation.115 | convolution fusion | flops 207617536 | bytes 3681792 | tf_op jit(solution)/shard_map/dot_general | solution.py:52
  70.4 4.0 %fusion.75 = (f32[512]{0:T(512)S(1)}, f32[512,1536]{0,1:T(8,128)}) fusion(bf16[512,512]{1,0:T(8,128)(2,1)} %bitcast.71, bf16[1536,256]{1,0:T(8,128)(2,1)S(1)} %copy-done.11, pred[1536]{0:T(1024)(128)(4,1)S(1)} %broadcast_compare_fusion, s32[1536]{0:T(1024)S(1)} %iota_add_fusion, s32[512]{0:T(512)S(1)} %iota_add_fusion.1), kind=kOutput, calls=%fused_computation.116 | convolution fusion | flops 207617536 | bytes 3684352 | tf_op jit(solution)/shard_map/dot_general | solution.py:52
  74.3 2.8 %all-to-all-done.3 = bf16[128,4,512]{0,2,1:T(8,128)(2,1)} async-done(((bf16[128,4,512]{0,2,1:T(8,128)(2,1)}), bf16[128,4,512]{0,2,1:T(8,128)(2,1)}, u32[]{:S(2)}, u32[]{:S(2)}) %all-to-all-start.3) | async-done | bytes 524320 | tf_op jit(solution)/shard_map/all_to_all | solution.py:27
  77.1 2.0 %copy.31 = bf16[4,128,512]{2,1,0:T(8,128)(2,1)} copy(bf16[4,128,512]{1,2,0:T(8,128)(2,1)} %bitcast.11) | data formatting | bytes 1048576 | tf_op jit(solution)/shard_map/all_to_all | solution.py:27
  79.2 2.5 %fusion.15 = f32[512]{0:T(512)S(1)} fusion(f32[512,1536]{0,1:T(8,128)} %get-tuple-element.15, f32[512]{0:T(512)S(1)} %get-tuple-element.14), kind=kLoop, calls=%fused_computation.37 | loop fusion | flops 1572352 | bytes 3149824 | tf_op jit(solution)/shard_map/reduce_sum | solution.py:58
  96.8 1.9 %collective-permute-start.6 = (bf16[512,256]{0,1:T(8,128)(2,1)S(1)}, bf16[512,256]{0,1:T(8,128)(2,1)S(1)}, u32[]{:S(2)}, u32[]{:S(2)}) collective-permute-start(bf16[512,256]{0,1:T(8,128)(2,1)S(1)} %get-tuple-element.6), channel_id=1, source_target_pairs={{4,0},{8,4},{12,8},{16,12},{20,16},{24,20},{28,24},{32,28},{36,32}... | collective-permute-start | bytes 786440 | tf_op jit(solution)/shard_map/ppermute | solution.py:19
  98.7 10.4 %collective-permute-start.7 = (bf16[512,256]{0,1:T(8,128)(2,1)S(1)}, bf16[512,256]{0,1:T(8,128)(2,1)S(1)}, u32[]{:S(2)}, u32[]{:S(2)}) collective-permute-start(bf16[512,256]{0,1:T(8,128)(2,1)S(1)} %get-tuple-element.7), channel_id=1, source_target_pairs={{8,0},{12,4},{16,8},{20,12},{24,16},{28,20},{32,24},{36,28},{40,32... | collective-permute-start | bytes 786440 | tf_op jit(solution)/shard_map/ppermute | solution.py:19
  113.1 1.9 %collective-permute-start.4 = (bf16[512,256]{0,1:T(8,128)(2,1)}, bf16[512,256]{0,1:T(8,128)(2,1)}, u32[]{:S(2)}, u32[]{:S(2)}) collective-permute-start(bf16[512,256]{0,1:T(8,128)(2,1)} %get-tuple-element.8), channel_id=1, source_target_pairs={{4,0},{8,4},{12,8},{16,12},{20,16},{24,20},{28,24},{32,28},{36,32}... | collective-permute-start | bytes 786440 | tf_op jit(solution)/shard_map/ppermute | solution.py:19
  115.1 2.2 %collective-permute-start.5 = (bf16[512,256]{0,1:T(8,128)(2,1)}, bf16[512,256]{0,1:T(8,128)(2,1)}, u32[]{:S(2)}, u32[]{:S(2)}) collective-permute-start(bf16[512,256]{0,1:T(8,128)(2,1)} %get-tuple-element.9), channel_id=1, source_target_pairs={{8,0},{12,4},{16,8},{20,12},{24,16},{28,20},{32,24},{36,28},{40,32... | collective-permute-start | bytes 786440 | tf_op jit(solution)/shard_map/ppermute | solution.py:19
  119.2 5.7 %all-to-all-start.6 = ((bf16[4,128,256]{1,2,0:T(8,128)(2,1)}), bf16[4,128,256]{1,2,0:T(8,128)(2,1)S(1)}, u32[]{:S(2)}, u32[]{:S(2)}) async-start(bf16[4,128,256]{1,2,0:T(8,128)(2,1)} %copy_bitcast_fusion.1), calls=%async_computation.6 | async-start | bytes 524288 | tf_op jit(solution)/shard_map/all_to_all | solution.py:98
  124.8 2.5 %convolution_convert_fusion.3 = bf16[512,128]{0,1:T(8,128)(2,1)} fusion(bf16[512,1536]{0,1:T(8,128)(2,1)} %copy-done.7, bf16[1536,256]{1,0:T(8,128)(2,1)} %copy-done.10), kind=kOutput, calls=%fused_computation.61 | convolution fusion | flops 201392128 | bytes 2097152 | tf_op jit(solution)/shard_map/dot_general | solution.py:66
  127.4 1.8 %copy_bitcast_fusion.2 = bf16[4,128,256]{1,2,0:T(8,128)(2,1)} fusion(bf16[512,256]{0,1:T(8,128)(2,1)} %collective-permute-done.5, bf16[512,256]{0,1:T(8,128)(2,1)} %collective-permute-done.4, f32[1536,128]{0,1:T(8,128)S(1)} %copy-done.4, f32[1536,128]{0,1:T(8,128)S(1)} %convolution_add_fusion.3), kind=kLoop, calls=%fused_computation.79 | loop fusion | flops 786432 | bytes 2359296 | tf_op jit(solution)/shard_map/all_to_all | solution.py:97
  129.2 6.7 %all-to-all-done.6 = bf16[4,128,256]{1,2,0:T(8,128)(2,1)S(1)} async-done(((bf16[4,128,256]{1,2,0:T(8,128)(2,1)}), bf16[4,128,256]{1,2,0:T(8,128)(2,1)S(1)}, u32[]{:S(2)}, u32[]{:S(2)}) %all-to-all-start.6) | async-done | bytes 262176 | tf_op jit(solution)/shard_map/all_to_all | solution.py:98
  135.9 3.4 %all-to-all-start.5 = ((bf16[4,128,256]{1,2,0:T(8,128)(2,1)}), bf16[4,128,256]{1,2,0:T(8,128)(2,1)S(1)}, u32[]{:S(2)}, u32[]{:S(2)}) async-start(bf16[4,128,256]{1,2,0:T(8,128)(2,1)} %copy_bitcast_fusion.2), calls=%async_computation.5 | async-start | bytes 524288 | tf_op jit(solution)/shard_map/all_to_all | solution.py:97
  140.8 1.9 %copy_bitcast_fusion = bf16[4,128,512]{1,2,0:T(8,128)(2,1)} fusion(bf16[512,128]{0,1:T(8,128)(2,1)S(1)} %convolution_convert_fusion, bf16[512,128]{0,1:T(8,128)(2,1)} %convolution_convert_fusion.1, bf16[512,128]{0,1:T(8,128)(2,1)S(1)} %convolution_convert_fusion.2, bf16[512,128]{0,1:T(8,128)(2,1)} %convolution_convert_fusion.3), kind=kLoop, calls=%fused_computation.72 | loop fusion | flops 2097152 | bytes 1048576 | tf_op jit(solution)/shard_map/all_to_all | solution.py:96
  142.6 10.3 %all-to-all-done.5 = bf16[4,128,256]{1,2,0:T(8,128)(2,1)S(1)} async-done(((bf16[4,128,256]{1,2,0:T(8,128)(2,1)}), bf16[4,128,256]{1,2,0:T(8,128)(2,1)S(1)}, u32[]{:S(2)}, u32[]{:S(2)}) %all-to-all-start.5) | async-done | bytes 262176 | tf_op jit(solution)/shard_map/all_to_all | solution.py:97
  152.9 5.0 %all-to-all-start.4 = ((bf16[4,128,512]{1,2,0:T(8,128)(2,1)}), bf16[4,128,512]{1,2,0:T(8,128)(2,1)S(1)}, u32[]{:S(2)}, u32[]{:S(2)}) async-start(bf16[4,128,512]{1,2,0:T(8,128)(2,1)} %copy_bitcast_fusion), calls=%async_computation.4 | async-start | bytes 1048576 | tf_op jit(solution)/shard_map/all_to_all | solution.py:96
  159.6 8.8 %all-to-all-done.4 = bf16[4,128,512]{1,2,0:T(8,128)(2,1)S(1)} async-done(((bf16[4,128,512]{1,2,0:T(8,128)(2,1)}), bf16[4,128,512]{1,2,0:T(8,128)(2,1)S(1)}, u32[]{:S(2)}, u32[]{:S(2)}) %all-to-all-start.4) | async-done | bytes 524320 | tf_op jit(solution)/shard_map/all_to_all | solution.py:96
  (81 shorter events, 31.1 us)
Async XLA Ops:
  0.6 46.1 %copy-start.14 = (bf16[128,2048]{1,0:T(8,128)(2,1)S(1)}, bf16[128,2048]{1,0:T(8,128)(2,1)}, u32[]{:S(2)}) copy-start(bf16[128,2048]{1,0:T(8,128)(2,1)} %param.7) | copy-start | bytes 1572868
  2.5 16.2 %all-to-all-start.2 = ((bf16[128,4,256]{0,2,1:T(8,128)(2,1)}), bf16[128,4,256]{0,2,1:T(8,128)(2,1)S(1)}, u32[]{:S(2)}, u32[]{:S(2)}) async-start(bf16[128,4,256]{0,2,1:T(8,128)(2,1)} %bitcast.7), calls=%async_computation.2 | async-start | bytes 524288 | tf_op jit(solution)/shard_map/all_to_all | solution.py:26
  18.7 14.1 %all-to-all-start = ((bf16[128,4,256]{0,2,1:T(8,128)(2,1)}), bf16[128,4,256]{0,2,1:T(8,128)(2,1)S(1)}, u32[]{:S(2)}, u32[]{:S(2)}) async-start(bf16[128,4,256]{0,2,1:T(8,128)(2,1)} %bitcast), calls=%async_computation | async-start | bytes 524288 | tf_op jit(solution)/shard_map/all_to_all | solution.py:25
  24.7 23.1 %collective-permute-start.3 = (bf16[512,256]{1,0:T(8,128)(2,1)S(1)}, bf16[512,256]{1,0:T(8,128)(2,1)S(1)}, u32[]{:S(2)}, u32[]{:S(2)}) collective-permute-start(bf16[512,256]{1,0:T(8,128)(2,1)S(1)} %bitcast.82), channel_id=1, source_target_pairs={{0,4},{4,8},{8,12},{12,16},{16,20},{20,24},{24,28},{28,32},{32,36}... | collective-permute-start | bytes 786440 | tf_op jit(solution)/shard_map/ppermute | solution.py:19
  26.6 21.1 %collective-permute-start.2 = (bf16[512,256]{1,0:T(8,128)(2,1)S(1)}, bf16[512,256]{1,0:T(8,128)(2,1)S(1)}, u32[]{:S(2)}, u32[]{:S(2)}) collective-permute-start(bf16[512,256]{1,0:T(8,128)(2,1)S(1)} %bitcast.83), channel_id=1, source_target_pairs={{0,8},{4,12},{8,16},{12,20},{16,24},{20,28},{24,32},{28,36},{32,40... | collective-permute-start | bytes 786440 | tf_op jit(solution)/shard_map/ppermute | solution.py:19
  32.7 21.4 %all-to-all-start.1 = ((bf16[128,4,512]{0,2,1:T(8,128)(2,1)}), bf16[128,4,512]{0,2,1:T(8,128)(2,1)S(1)}, u32[]{:S(2)}, u32[]{:S(2)}) async-start(bf16[128,4,512]{0,2,1:T(8,128)(2,1)} %bitcast.3), calls=%async_computation.1 | async-start | bytes 1048576 | tf_op jit(solution)/shard_map/all_to_all | solution.py:24
  38.3 10.4 %collective-permute-start.1 = (bf16[512,256]{1,0:T(8,128)(2,1)S(1)}, bf16[512,256]{1,0:T(8,128)(2,1)S(1)}, u32[]{:S(2)}, u32[]{:S(2)}) collective-permute-start(bf16[512,256]{1,0:T(8,128)(2,1)S(1)} %bitcast.85), channel_id=1, source_target_pairs={{0,4},{4,8},{8,12},{12,16},{16,20},{20,24},{24,28},{28,32},{32,36}... | collective-permute-start | bytes 786440 | tf_op jit(solution)/shard_map/ppermute | solution.py:19
  43.4 10.7 %collective-permute-start = (bf16[512,256]{1,0:T(8,128)(2,1)S(1)}, bf16[512,256]{1,0:T(8,128)(2,1)S(1)}, u32[]{:S(2)}, u32[]{:S(2)}) collective-permute-start(bf16[512,256]{1,0:T(8,128)(2,1)S(1)} %bitcast.86), channel_id=1, source_target_pairs={{0,8},{4,12},{8,16},{12,20},{16,24},{20,28},{24,32},{28,36},{32,40... | collective-permute-start | bytes 786440 | tf_op jit(solution)/shard_map/ppermute | solution.py:19
  54.1 10.5 %copy-start.10 = (bf16[1536,256]{1,0:T(8,128)(2,1)}, bf16[1536,256]{1,0:T(8,128)(2,1)S(1)}, u32[]{:S(2)}) copy-start(bf16[1536,256]{1,0:T(8,128)(2,1)S(1)} %pad_maximum_fusion.2) | copy-start | bytes 2359300
  54.1 23.0 %all-to-all-start.3 = ((bf16[128,4,512]{0,2,1:T(8,128)(2,1)}), bf16[128,4,512]{0,2,1:T(8,128)(2,1)}, u32[]{:S(2)}, u32[]{:S(2)}) async-start(bf16[128,4,512]{0,2,1:T(8,128)(2,1)} %bitcast.10), calls=%async_computation.3 | async-start | bytes 1048576 | tf_op jit(solution)/shard_map/all_to_all | solution.py:27
  61.5 3.1 %copy-start.8 = (bf16[4,128,512]{2,1,0:T(8,128)(2,1)}, bf16[4,128,512]{2,1,0:T(8,128)(2,1)S(1)}, u32[]{:S(2)}) copy-start(bf16[4,128,512]{2,1,0:T(8,128)(2,1)S(1)} %copy.27) | copy-start | bytes 1572868
  67.7 2.6 %copy-start.11 = (bf16[1536,256]{1,0:T(8,128)(2,1)S(1)}, bf16[1536,256]{1,0:T(8,128)(2,1)}, u32[]{:S(2)}) copy-start(bf16[1536,256]{1,0:T(8,128)(2,1)} %copy-done.10) | copy-start | bytes 2359300
  79.2 2.8 %copy-start.1 = (f32[512,1536]{0,1:T(8,128)S(1)}, f32[512,1536]{0,1:T(8,128)}, u32[]{:S(2)}) copy-start(f32[512,1536]{0,1:T(8,128)} %get-tuple-element.15) | copy-start | bytes 9437188
  82.0 1.8 %copy-start.13 = (bf16[1536,256]{1,0:T(8,128)(2,1)S(1)}, bf16[1536,256]{1,0:T(8,128)(2,1)}, u32[]{:S(2)}) copy-start(bf16[1536,256]{1,0:T(8,128)(2,1)} %pad_maximum_fusion.3) | copy-start | bytes 2359300
  82.0 1.8 %copy-start.15 = (bf16[4,128,512]{2,1,0:T(8,128)(2,1)S(1)}, bf16[4,128,512]{2,1,0:T(8,128)(2,1)}, u32[]{:S(2)}) copy-start(bf16[4,128,512]{2,1,0:T(8,128)(2,1)} %copy.31) | copy-start | bytes 1572868
  83.8 1.9 %copy-start = (f32[512,1536]{0,1:T(8,128)S(1)}, f32[512,1536]{0,1:T(8,128)}, u32[]{:S(2)}) copy-start(f32[512,1536]{0,1:T(8,128)} %get-tuple-element.23) | copy-start | bytes 9437188
  86.9 1.9 %copy-start.2 = (f32[512,1536]{0,1:T(8,128)S(1)}, f32[512,1536]{0,1:T(8,128)}, u32[]{:S(2)}) copy-start(f32[512,1536]{0,1:T(8,128)} %get-tuple-element.11) | copy-start | bytes 9437188
  90.0 1.1 copy-start.12
  92.3 1.0 copy-start.9
  94.7 17.5 %copy-start.3 = (f32[1536,128]{0,1:T(8,128)}, f32[1536,128]{0,1:T(8,128)S(1)}, u32[]{:S(2)}) copy-start(f32[1536,128]{0,1:T(8,128)S(1)} %convolution_add_fusion.2) | copy-start | bytes 2359300
  96.8 21.6 %collective-permute-start.6 = (bf16[512,256]{0,1:T(8,128)(2,1)S(1)}, bf16[512,256]{0,1:T(8,128)(2,1)S(1)}, u32[]{:S(2)}, u32[]{:S(2)}) collective-permute-start(bf16[512,256]{0,1:T(8,128)(2,1)S(1)} %get-tuple-element.6), channel_id=1, source_target_pairs={{4,0},{8,4},{12,8},{16,12},{20,16},{24,20},{28,24},{32,28},{36,32}... | collective-permute-start | bytes 786440 | tf_op jit(solution)/shard_map/ppermute | solution.py:19
  98.7 19.6 %collective-permute-start.7 = (bf16[512,256]{0,1:T(8,128)(2,1)S(1)}, bf16[512,256]{0,1:T(8,128)(2,1)S(1)}, u32[]{:S(2)}, u32[]{:S(2)}) collective-permute-start(bf16[512,256]{0,1:T(8,128)(2,1)S(1)} %get-tuple-element.7), channel_id=1, source_target_pairs={{8,0},{12,4},{16,8},{20,12},{24,16},{28,20},{32,24},{36,28},{40,32... | collective-permute-start | bytes 786440 | tf_op jit(solution)/shard_map/ppermute | solution.py:19
  110.0 1.5 copy-start.7
  111.5 1.6 copy-start.5
  113.1 14.2 %collective-permute-start.4 = (bf16[512,256]{0,1:T(8,128)(2,1)}, bf16[512,256]{0,1:T(8,128)(2,1)}, u32[]{:S(2)}, u32[]{:S(2)}) collective-permute-start(bf16[512,256]{0,1:T(8,128)(2,1)} %get-tuple-element.8), channel_id=1, source_target_pairs={{4,0},{8,4},{12,8},{16,12},{20,16},{24,20},{28,24},{32,28},{36,32}... | collective-permute-start | bytes 786440 | tf_op jit(solution)/shard_map/ppermute | solution.py:19
  115.1 12.3 %collective-permute-start.5 = (bf16[512,256]{0,1:T(8,128)(2,1)}, bf16[512,256]{0,1:T(8,128)(2,1)}, u32[]{:S(2)}, u32[]{:S(2)}) collective-permute-start(bf16[512,256]{0,1:T(8,128)(2,1)} %get-tuple-element.9), channel_id=1, source_target_pairs={{8,0},{12,4},{16,8},{20,12},{24,16},{28,20},{32,24},{36,28},{40,32... | collective-permute-start | bytes 786440 | tf_op jit(solution)/shard_map/ppermute | solution.py:19
  118.4 9.0 %copy-start.4 = (f32[1536,128]{0,1:T(8,128)S(1)}, f32[1536,128]{0,1:T(8,128)}, u32[]{:S(2)}) copy-start(f32[1536,128]{0,1:T(8,128)} %copy-done.3) | copy-start | bytes 2359300
  119.2 20.2 %copy-start.6 = (bf16[512,1536]{0,1:T(8,128)(2,1)S(1)}, bf16[512,1536]{0,1:T(8,128)(2,1)}, u32[]{:S(2)}) copy-start(bf16[512,1536]{0,1:T(8,128)(2,1)} %copy-done.5) | copy-start | bytes 4718596
  119.2 16.8 %all-to-all-start.6 = ((bf16[4,128,256]{1,2,0:T(8,128)(2,1)}), bf16[4,128,256]{1,2,0:T(8,128)(2,1)S(1)}, u32[]{:S(2)}, u32[]{:S(2)}) async-start(bf16[4,128,256]{1,2,0:T(8,128)(2,1)} %copy_bitcast_fusion.1), calls=%async_computation.6 | async-start | bytes 524288 | tf_op jit(solution)/shard_map/all_to_all | solution.py:98
  135.9 17.0 %all-to-all-start.5 = ((bf16[4,128,256]{1,2,0:T(8,128)(2,1)}), bf16[4,128,256]{1,2,0:T(8,128)(2,1)S(1)}, u32[]{:S(2)}, u32[]{:S(2)}) async-start(bf16[4,128,256]{1,2,0:T(8,128)(2,1)} %copy_bitcast_fusion.2), calls=%async_computation.5 | async-start | bytes 524288 | tf_op jit(solution)/shard_map/all_to_all | solution.py:97
  152.9 15.5 %all-to-all-start.4 = ((bf16[4,128,512]{1,2,0:T(8,128)(2,1)}), bf16[4,128,512]{1,2,0:T(8,128)(2,1)S(1)}, u32[]{:S(2)}, u32[]{:S(2)}) async-start(bf16[4,128,512]{1,2,0:T(8,128)(2,1)} %copy_bitcast_fusion), calls=%async_computation.4 | async-start | bytes 1048576 | tf_op jit(solution)/shard_map/all_to_all | solution.py:96
where the time goes:
time: 171 us; the launch traced here: 169 us
  starting transfers between devices  67.8 us (40%)
  waiting for transfers between devices  43.9 us (26%)
  matrix products  27.6 us (16%)
  local copies, waits for them, and re-layouts  15.9 us (9%)
  other arithmetic  13.1 us (8%)
    ppermute x8, starting transfers between devices, shifted(): lax.ppermute(value, axis, [(source, source + steps) for source in range(f...  31 us
    dot_general x4, matrix products, on_device(): lax.dot_general(query_head, key_head, contract_last, preferred_element_ty...  12.8 us
    unnamed x39, local copies, waits for them, and re-layouts  12.5 us
    all_to_all x1, waiting for transfers between devices, on_device(): lax.all_to_all(key_grad, 'head', split_axis=0, concat_axis=1, tiled=True)  10.3 us
    all_to_all x1, waiting for transfers between devices, on_device(): lax.all_to_all(query_grad, 'head', split_axis=0, concat_axis=1, tiled=True)  8.79 us
    all_to_all x1, waiting for transfers between devices, on_device(): lax.all_to_all(saved_value_rows, 'head', split_axis=1, concat_axis=0, til...  8.18 us
    all_to_all x1, starting transfers between devices, on_device(): lax.all_to_all(out_grad, 'head', split_axis=1, concat_axis=0, tiled=True)  7.21 us
    all_to_all x1, waiting for transfers between devices, on_device(): lax.all_to_all(value_grad, 'head', split_axis=0, concat_axis=1, tiled=True)  6.73 us
  transfers between devices with their start and end apart: 15, of which 7 were waited for; matrix products, arithmetic and copies ran while one was open for 20% of the time, Pallas kernels for 0%

commit v1 on v0

v1 whole, which is shorter than its diff:
```python
import jax
import jax.numpy as jnp
from jax import lax
from jax.experimental import pallas as pl
from jax.experimental.pallas import tpu as pltpu
from jax.sharding import PartitionSpec as P

HEAD_SIZE = 128
W = 1024
PEERS = 8
BLOCK = W // PEERS
QUERIES = 256
STEPS = W // QUERIES
CHUNK = 256
CHUNKS = (W + QUERIES) // CHUNK
MESH = pl.DeviceIdType.MESH

score_scale = 168.0 ** (-0.5)
masked_value = -1e30
contract_last = (((1,), (1,)), ((), ()))

OTHERS = ((1, 0), (3, 0), (2, 0), (1, 1), (3, 1), (2, 1), (0, 1))
K, V, Q0, G0, Q1, G1 = range(6)


def kernel(
    query_in,
    key_in,
    value_in,
    grad_in,
    query_out,
    key_out,
    value_out,
    keys,
    values,
    keys_t,
    queries,
    grads,
    key_sum,
    value_sum,
    query_stage,
    back_stage,
    back_landing,
    own_stage,
    score_buf,
    prob_buf,
    in_send,
    in_recv,
    halo_send,
    halo_recv,
    query_send,
    query_recv,
    back_send,
    back_recv,
    own_send,
    own_recv,
):
    seq_count = lax.axis_size("seq")
    seq = lax.axis_index("seq")
    head = lax.axis_index("head")
    span = seq // 2
    core = seq % 2
    me = core * 4 + head

    def peer(step):
        other_head = (head + step[0]) % 4
        other_core = (core + step[1]) % 2
        return other_core * 4 + other_head, {"seq": span * 2 + other_core, "head": other_head}

    peers = [peer(step) for step in OTHERS]
    following = {"seq": (seq + 2) % seq_count, "head": head}
    preceding = {"seq": (seq + seq_count - 2) % seq_count, "head": head}

    def rows(block, size=BLOCK):
        return pl.ds(pl.multiple_of(block * size, size), size)

    def columns(index):
        return pl.ds(pl.multiple_of(index * HEAD_SIZE, HEAD_SIZE), HEAD_SIZE)

    def source(kind, home):
        if kind == K:
            return key_in.at[:, columns(home)]
        if kind == V:
            return value_in.at[:, columns(home)]
        array = query_in if kind in (Q0, Q1) else grad_in
        return array.at[:, columns(2 * home + (1 if kind in (Q1, G1) else 0))]

    def landing(kind, block):
        if kind == K:
            return keys.at[rows(PEERS + block)]
        if kind == V:
            return values.at[rows(PEERS + block)]
        array = queries if kind in (Q0, Q1) else grads
        return array.at[1 if kind in (Q1, G1) else 0, rows(block)]

    def local_in(kind):
        return pltpu.make_async_copy(source(kind, me), landing(kind, me), in_recv.at[kind, me])

    def remote_in(kind, index, device, block):
        return pltpu.make_async_remote_copy(
            src_ref=source(kind, index),
            dst_ref=landing(kind, block),
            send_sem=in_send.at[kind, index],
            recv_sem=in_recv.at[kind, block],
            device_id=device,
            device_id_type=MESH,
        )

    def wait_in(kind):
        for index, device in peers:
            remote_in(kind, index, device, index).wait_recv()
        local_in(kind).wait()

    for kind in (K, V, Q0, G0, Q1, G1):
        local_in(kind).start()

    barrier = pltpu.get_barrier_semaphore()
    for device in [device for _, device in peers] + [following, preceding]:
        pl.semaphore_signal(barrier, inc=1, device_id=device, device_id_type=MESH)
    pl.semaphore_wait(barrier, len(OTHERS) + 2)

    for kind in (K, V, Q0, G0, Q1, G1):
        for index, device in peers:
            remote_in(kind, index, device, me).start()

    key_sum[...] = jnp.zeros_like(key_sum)
    value_sum[...] = jnp.zeros_like(value_sum)

    def halo(which):
        array = keys if which == 0 else values
        return pltpu.make_async_remote_copy(
            src_ref=array.at[pl.ds(W, W)],
            dst_ref=array.at[pl.ds(0, W)],
            send_sem=halo_send.at[which],
            recv_sem=halo_recv.at[which],
            device_id=following,
            device_id_type=MESH,
        )

    wait_in(K)
    halo(0).start()
    wait_in(V)
    halo(1).start()
    halo(0).wait_recv()

    @pl.loop(0, 2 * W // CHUNK)
    def _(chunk):
        keys_t[chunk] = keys[rows(chunk, CHUNK), :].T

    halo(1).wait_recv()

    key_row = lax.broadcasted_iota(jnp.int32, (CHUNK, QUERIES), 0)
    query_row = lax.broadcasted_iota(jnp.int32, (CHUNK, QUERIES), 1)

    def compute(q_head, step):
        query = queries[q_head, rows(step, QUERIES), :]
        grad = grads[q_head, rows(step, QUERIES), :]
        peak = None
        for part in range(CHUNKS):
            scores = (
                lax.dot_general(
                    keys[rows(step + part, CHUNK), :],
                    query,
                    contract_last,
                    preferred_element_type=jnp.float32,
                )
                * score_scale
            )
            if part < CHUNKS - 1:
                absent = (span == 0) & (step + part < W // CHUNK)
                scores = scores + jnp.where(absent, masked_value, 0.0)
            if part == 0:
                scores = jnp.where(key_row > query_row, scores, masked_value)
            if part == CHUNKS - 1:
                scores = jnp.where(key_row <= query_row, scores, masked_value)
            score_buf[part] = scores
            top = jnp.max(scores, axis=0, keepdims=True)
            peak = top if peak is None else jnp.maximum(peak, top)
        total = jnp.zeros((1, QUERIES), jnp.float32)
        delta = jnp.zeros((1, QUERIES), jnp.float32)
        for part in range(CHUNKS):
            weights = jnp.exp(score_buf[part] - peak)
            prob_grad = lax.dot_general(
                values[rows(step + part, CHUNK), :],
                grad,
                contract_last,
                preferred_element_type=jnp.float32,
            )
            score_buf[part] = weights
            prob_buf[part] = prob_grad
            total = total + jnp.sum(weights, axis=0, keepdims=True)
            delta = delta + jnp.sum(weights * prob_grad, axis=0, keepdims=True)
        inverse = 1.0 / total
        delta = delta * inverse
        query_grad = jnp.zeros((HEAD_SIZE, QUERIES), jnp.float32)
        for part in range(CHUNKS):
            attention = score_buf[part] * inverse
            score_grad = (score_scale * attention * (prob_buf[part] - delta)).astype(jnp.bfloat16)
            at = rows(step + part, CHUNK)
            value_sum[at, :] += jnp.dot(
                attention.astype(jnp.bfloat16), grad, preferred_element_type=jnp.float32
            )
            key_sum[at, :] += jnp.dot(score_grad, query, preferred_element_type=jnp.float32)
            query_grad = query_grad + jnp.dot(
                keys_t[step + part], score_grad, preferred_element_type=jnp.float32
            )
        query_stage[q_head, rows(step, QUERIES), :] = query_grad.T.astype(jnp.bfloat16)

    def query_local(q_head):
        return pltpu.make_async_copy(
            query_stage.at[q_head, rows(me)],
            query_out.at[:, columns(2 * me + q_head)],
            query_recv.at[q_head, me],
        )

    def query_remote(q_head, index, device, home):
        return pltpu.make_async_remote_copy(
            src_ref=query_stage.at[q_head, rows(index)],
            dst_ref=query_out.at[:, columns(2 * home + q_head)],
            send_sem=query_send.at[q_head, index],
            recv_sem=query_recv.at[q_head, home],
            device_id=device,
            device_id_type=MESH,
        )

    def send_query(q_head):
        query_local(q_head).start()
        for index, device in peers:
            query_remote(q_head, index, device, me).start()

    def back(which, step):
        return pltpu.make_async_remote_copy(
            src_ref=back_stage.at[which, rows(step, QUERIES)],
            dst_ref=back_landing.at[which, rows(step, QUERIES)],
            send_sem=back_send.at[which, step],
            recv_sem=back_recv.at[which, step],
            device_id=preceding,
            device_id_type=MESH,
        )

    wait_in(Q0)
    wait_in(G0)

    @pl.loop(0, STEPS)
    def _(step):
        compute(0, step)

    wait_in(Q1)
    wait_in(G1)
    send_query(0)

    @pl.loop(0, STEPS)
    def _(step):
        compute(1, step)
        at = rows(step, QUERIES)
        back_stage[0, at, :] = key_sum[at, :].astype(jnp.bfloat16)
        back_stage[1, at, :] = value_sum[at, :].astype(jnp.bfloat16)
        back(0, step).start()
        back(1, step).start()

    send_query(1)

    def own_out(which):
        return key_out if which == 0 else value_out

    def own_local(which):
        return pltpu.make_async_copy(
            own_stage.at[which, rows(me)],
            own_out(which).at[:, columns(me)],
            own_recv.at[which, me],
        )

    def own_remote(which, index, device, home):
        return pltpu.make_async_remote_copy(
            src_ref=own_stage.at[which, rows(index)],
            dst_ref=own_out(which).at[:, columns(home)],
            send_sem=own_send.at[which, index],
            recv_sem=own_recv.at[which, home],
            device_id=device,
            device_id_type=MESH,
        )

    @pl.loop(0, STEPS)
    def _(step):
        at = rows(step, QUERIES)
        own = rows(STEPS + step, QUERIES)
        for which, sums in ((0, key_sum), (1, value_sum)):
            back(which, step).wait_recv()
            own_stage[which, at, :] = (
                sums[own, :] + back_landing[which, at, :].astype(jnp.float32)
            ).astype(jnp.bfloat16)

    for which in (0, 1):
        own_local(which).start()
        for index, device in peers:
            own_remote(which, index, device, me).start()

    for kind in (K, V, Q0, G0, Q1, G1):
        for index, device in peers:
            remote_in(kind, index, device, me).wait_send()
    for which in (0, 1):
        halo(which).wait_send()
        for step in range(STEPS):
            back(which, step).wait_send()
        query_local(which).wait()
        own_local(which).wait()
        for index, device in peers:
            query_remote(which, index, device, me).wait_send()
            query_remote(which, index, device, index).wait_recv()
            own_remote(which, index, device, me).wait_send()
            own_remote(which, index, device, index).wait_recv()


def on_device(query_rows, key_rows, saved_value_rows, out_grad):
    dma = pltpu.SemaphoreType.DMA
    low, wide = jnp.bfloat16, jnp.float32
    anywhere = pl.BlockSpec(memory_space=pl.ANY)
    return pl.pallas_call(
        kernel,
        out_shape=(
            jax.ShapeDtypeStruct(query_rows.shape, low),
            jax.ShapeDtypeStruct(key_rows.shape, low),
            jax.ShapeDtypeStruct(saved_value_rows.shape, low),
        ),
        in_specs=[anywhere] * 4,
        out_specs=(anywhere,) * 3,
        scratch_shapes=[
            pltpu.VMEM((2 * W, HEAD_SIZE), low),
            pltpu.VMEM((2 * W, HEAD_SIZE), low),
            pltpu.VMEM((2 * W // CHUNK, HEAD_SIZE, CHUNK), low),
            pltpu.VMEM((2, W, HEAD_SIZE), low),
            pltpu.VMEM((2, W, HEAD_SIZE), low),
            pltpu.VMEM((2 * W, HEAD_SIZE), wide),
            pltpu.VMEM((2 * W, HEAD_SIZE), wide),
            pltpu.VMEM((2, W, HEAD_SIZE), low),
            pltpu.VMEM((2, W, HEAD_SIZE), low),
            pltpu.VMEM((2, W, HEAD_SIZE), low),
            pltpu.VMEM((2, W, HEAD_SIZE), low),
            pltpu.VMEM((CHUNKS, CHUNK, QUERIES), wide),
            pltpu.VMEM((CHUNKS, CHUNK, QUERIES), wide),
            dma((6, PEERS)),
            dma((6, PEERS)),
            dma((2,)),
            dma((2,)),
            dma((2, PEERS)),
            dma((2, PEERS)),
            dma((2, STEPS)),
            dma((2, STEPS)),
            dma((2, PEERS)),
            dma((2, PEERS)),
        ],
        compiler_params=pltpu.CompilerParams(collective_id=0, has_side_effects=True),
        name="attention_backward",
    )(query_rows, key_rows, saved_value_rows, out_grad)


def solution(mesh):
    rows_split = P(("seq", "head"), None)
    return jax.shard_map(
        on_device,
        mesh=mesh,
        in_specs=(rows_split,) * 4,
        out_specs=(rows_split,) * 3,
        check_vma=False,
    )
```

time: 171 us -> 113 us (0.66)
  the two profiles are of different devices: /device:TPU:136 before, /device:TPU:1 now
where the time goes in v1:
time: 113 us
  Pallas kernels  109 us (96%)
  local copies, waits for them, and re-layouts  3.67 us (3%)
    pallas_call x1, Pallas kernels, on_device(): pl.pallas_call(kernel, out_shape=(jax.ShapeDtypeStruct(query_rows.shape,...  109 us
    unnamed x7, local copies, waits for them, and re-layouts  3.67 us

profile of v1, /device:TPU:1, one launch (start us, length us, event | category | flops | bytes accessed | tf_op | source)
XLA Modules:
  0.0 113.3 jit_solution(7100810863126666046)
XLA Ops:
  0.6 108.9 %attention_backward.1 = (bf16[128,2048]{1,0:T(8,128)(2,1)}, bf16[128,1024]{1,0:T(8,128)(2,1)}, bf16[128,1024]{1,0:T(8,128)(2,1)}) custom-call(bf16[128,2048]{1,0:T(8,128)(2,1)} %query_in.1, bf16[128,1024]{1,0:T(8,128)(2,1)} %key_in.1, bf16[128,1024]{1,0:T(8,128)(2,1)} %value_in.1, bf16[128,2048]{1,0:T(8,128)(2,1)} %grad_in.1), custom_call_target="tpu_custom_call" | custom-call | tf_op jit(solution)/shard_map/attention_backward/pallas_call | solution.py:318
  109.6 0.0 copy-start.1
  109.6 1.9 %copy.10 = bf16[128,2048]{1,0:T(8,128)(2,1)} copy(bf16[128,2048]{1,0:T(8,128)(2,1)} %get-tuple-element.6) | data formatting | bytes 1048576
  111.5 0.0 copy-done.1
  111.5 0.0 copy-start
  111.5 0.7 copy.11
  112.2 0.3 copy-done
  112.6 0.7 copy.12
Async XLA Ops:
  109.6 1.9 %copy-start.1 = (bf16[128,1024]{1,0:T(8,128)(2,1)S(1)}, bf16[128,1024]{1,0:T(8,128)(2,1)}, u32[]{:S(2)}) copy-start(bf16[128,1024]{1,0:T(8,128)(2,1)} %get-tuple-element.7) | copy-start | bytes 786436
  111.5 1.0 copy-start

commit v2 on v1

--- a/solution.py
+++ b/solution.py
@@ -7,8 +7,10 @@
 
 HEAD_SIZE = 128
 W = 1024
-PEERS = 8
-BLOCK = W // PEERS
+BLOCKS = 8
+BLOCK = W // BLOCKS
+LINE = 8
+DEPTH = 8
 QUERIES = 256
 STEPS = W // QUERIES
 CHUNK = 256
@@ -19,8 +21,9 @@
 masked_value = -1e30
 contract_last = (((1,), (1,)), ((), ()))
 
-OTHERS = ((1, 0), (3, 0), (2, 0), (1, 1), (3, 1), (2, 1), (0, 1))
-K, V, Q0, G0, Q1, G1 = range(6)
+HOMES = (1, 7, 2, 6, 3, 5, 4)
+OWNERS = ((0, 1), (1, 1), (0, 3), (1, 3), (0, 2), (1, 2), (1, 0))
+KINDS = K, V, Q0, G0, Q1, G1 = range(6)
 
 
 def kernel(
@@ -55,21 +58,36 @@
     own_send,
     own_recv,
 ):
-    seq_count = lax.axis_size("seq")
     seq = lax.axis_index("seq")
     head = lax.axis_index("head")
-    span = seq // 2
     core = seq % 2
-    me = core * 4 + head
-
-    def peer(step):
-        other_head = (head + step[0]) % 4
-        other_core = (core + step[1]) % 2
-        return other_core * 4 + other_head, {"seq": span * 2 + other_core, "head": other_head}
-
-    peers = [peer(step) for step in OTHERS]
-    following = {"seq": (seq + 2) % seq_count, "head": head}
-    preceding = {"seq": (seq + seq_count - 2) % seq_count, "head": head}
+    z = seq // 2 % DEPTH
+    y_lo = seq // (2 * DEPTH) % 2
+    x = seq // (4 * DEPTH)
+    y = head * 2 + y_lo
+    mine = core * 4 + head
+    alone = core == y_lo
+    span = (x * 2 + core) * DEPTH + z
+    span_count = lax.axis_size("seq") // 2
+
+    def chip(other_y, other_core):
+        other = (x * 2 + other_y % 2) * (2 * DEPTH) + z * 2 + other_core
+        return {"seq": other, "head": other_y // 2}
+
+    def span_home(other):
+        place = (other // (2 * DEPTH) * 2 + y_lo) * (2 * DEPTH) + other % DEPTH * 2
+        return {"seq": place + other // DEPTH % 2, "head": head}
+
+    def owner(step):
+        block_core, place = (core + step[0]) % 2, (head + step[1]) % 4
+        return block_core * 4 + place, chip(place * 2 + core, block_core)
+
+    homes = [((y + step) % LINE, chip((y + step) % LINE, y_lo)) for step in HOMES]
+    owners = [owner(step) for step in OWNERS]
+    near_home = (y, chip(y, y_lo))
+    near_owner = owner((0, 0))
+    following = span_home((span + 1) % span_count)
+    preceding = span_home((span + span_count - 1) % span_count)
 
     def rows(block, size=BLOCK):
         return pl.ds(pl.multiple_of(block * size, size), size)
@@ -87,41 +105,59 @@
 
     def landing(kind, block):
         if kind == K:
-            return keys.at[rows(PEERS + block)]
+            return keys.at[rows(BLOCKS + block)]
         if kind == V:
-            return values.at[rows(PEERS + block)]
+            return values.at[rows(BLOCKS + block)]
         array = queries if kind in (Q0, Q1) else grads
         return array.at[1 if kind in (Q1, G1) else 0, rows(block)]
 
     def local_in(kind):
-        return pltpu.make_async_copy(source(kind, me), landing(kind, me), in_recv.at[kind, me])
-
-    def remote_in(kind, index, device, block):
+        return pltpu.make_async_copy(source(kind, y), landing(kind, mine), in_recv.at[kind, mine])
+
+    def remote_in(kind, home, device, block):
         return pltpu.make_async_remote_copy(
-            src_ref=source(kind, index),
+            src_ref=source(kind, home),
             dst_ref=landing(kind, block),
-            send_sem=in_send.at[kind, index],
+            send_sem=in_send.at[kind, home],
             recv_sem=in_recv.at[kind, block],
             device_id=device,
             device_id_type=MESH,
         )
 
     def wait_in(kind):
-        for index, device in peers:
-            remote_in(kind, index, device, index).wait_recv()
-        local_in(kind).wait()
-
-    for kind in (K, V, Q0, G0, Q1, G1):
-        local_in(kind).start()
+        for block, device in owners + [near_owner]:
+            remote_in(kind, y, device, block).wait_recv()
+
+    @pl.when(alone)
+    def _():
+        for kind in KINDS:
+            local_in(kind).start()
 
     barrier = pltpu.get_barrier_semaphore()
-    for device in [device for _, device in peers] + [following, preceding]:
+
+    def greet(device):
         pl.semaphore_signal(barrier, inc=1, device_id=device, device_id_type=MESH)
-    pl.semaphore_wait(barrier, len(OTHERS) + 2)
-
-    for kind in (K, V, Q0, G0, Q1, G1):
-        for index, device in peers:
-            remote_in(kind, index, device, me).start()
+
+    for _, device in homes:
+        greet(device)
+    for place in range(4):
+        greet(chip(place * 2 + core, 1 - y_lo))
+    greet(following)
+    greet(preceding)
+
+    @pl.when(jnp.logical_not(alone))
+    def _():
+        greet(near_home[1])
+
+    pl.semaphore_wait(barrier, len(homes) + 6 + jnp.where(alone, 0, 1))
+
+    for kind in KINDS:
+        for home, device in homes:
+            remote_in(kind, home, device, mine).start()
+
+        @pl.when(jnp.logical_not(alone))
+        def _():
+            remote_in(kind, *near_home, mine).start()
 
     key_sum[...] = jnp.zeros_like(key_sum)
     value_sum[...] = jnp.zeros_like(value_sum)
@@ -208,25 +244,32 @@
 
     def query_local(q_head):
         return pltpu.make_async_copy(
-            query_stage.at[q_head, rows(me)],
-            query_out.at[:, columns(2 * me + q_head)],
-            query_recv.at[q_head, me],
-        )
-
-    def query_remote(q_head, index, device, home):
+            query_stage.at[q_head, rows(mine)],
+            query_out.at[:, columns(2 * y + q_head)],
+            query_recv.at[q_head, y],
+        )
+
+    def query_remote(q_head, block, device, home):
         return pltpu.make_async_remote_copy(
-            src_ref=query_stage.at[q_head, rows(index)],
+            src_ref=query_stage.at[q_head, rows(block)],
             dst_ref=query_out.at[:, columns(2 * home + q_head)],
-            send_sem=query_send.at[q_head, index],
+            send_sem=query_send.at[q_head, block],
             recv_sem=query_recv.at[q_head, home],
             device_id=device,
             device_id_type=MESH,
         )
 
     def send_query(q_head):
-        query_local(q_head).start()
-        for index, device in peers:
-            query_remote(q_head, index, device, me).start()
+        for block, device in owners:
+            query_remote(q_head, block, device, y).start()
+
+        @pl.when(alone)
+        def _():
+            query_local(q_head).start()
+
+        @pl.when(jnp.logical_not(alone))
+        def _():
+            query_remote(q_head, *near_owner, y).start()
 
     def back(which, step):
         return pltpu.make_async_remote_copy(
@@ -265,16 +308,16 @@
 
     def own_local(which):
         return pltpu.make_async_copy(
-            own_stage.at[which, rows(me)],
-            own_out(which).at[:, columns(me)],
-            own_recv.at[which, me],
-        )
-
-    def own_remote(which, index, device, home):
+            own_stage.at[which, rows(mine)],
+            own_out(which).at[:, columns(y)],
+            own_recv.at[which, y],
+        )
+
+    def own_remote(which, block, device, home):
         return pltpu.make_async_remote_copy(
-            src_ref=own_stage.at[which, rows(index)],
+            src_ref=own_stage.at[which, rows(block)],
             dst_ref=own_out(which).at[:, columns(home)],
-            send_sem=own_send.at[which, index],
+            send_sem=own_send.at[which, block],
             recv_sem=own_recv.at[which, home],
             device_id=device,
             device_id_type=MESH,
@@ -291,24 +334,37 @@
             ).astype(jnp.bfloat16)
 
     for which in (0, 1):
-        own_local(which).start()
-        for index, device in peers:
-            own_remote(which, index, device, me).start()
-
-    for kind in (K, V, Q0, G0, Q1, G1):
-        for index, device in peers:
-            remote_in(kind, index, device, me).wait_send()
+        for block, device in owners:
+            own_remote(which, block, device, y).start()
+
+    @pl.when(alone)
+    def _():
+        for which in (0, 1):
+            own_local(which).start()
+
+    @pl.when(jnp.logical_not(alone))
+    def _():
+        for which in (0, 1):
+            own_remote(which, *near_owner, y).start()
+        for kind in KINDS:
+            remote_in(kind, *near_home, mine).wait_send()
+        for which in (0, 1):
+            query_remote(which, *near_owner, y).wait_send()
+            own_remote(which, *near_owner, y).wait_send()
+
+    for kind in KINDS:
+        for home, device in homes:
+            remote_in(kind, home, device, mine).wait_send()
     for which in (0, 1):
         halo(which).wait_send()
         for step in range(STEPS):
             back(which, step).wait_send()
-        query_local(which).wait()
-        own_local(which).wait()
-        for index, device in peers:
-            query_remote(which, index, device, me).wait_send()
-            query_remote(which, index, device, index).wait_recv()
-            own_remote(which, index, device, me).wait_send()
-            own_remote(which, index, device, index).wait_recv()
+        for block, device in owners:
+            query_remote(which, block, device, y).wait_send()
+            own_remote(which, block, device, y).wait_send()
+        for home, device in homes + [near_home]:
+            query_remote(which, mine, device, home).wait_recv()
+            own_remote(which, mine, device, home).wait_recv()
 
 
 def on_device(query_rows, key_rows, saved_value_rows, out_grad):
@@ -338,16 +394,16 @@
             pltpu.VMEM((2, W, HEAD_SIZE), low),
             pltpu.VMEM((CHUNKS, CHUNK, QUERIES), wide),
             pltpu.VMEM((CHUNKS, CHUNK, QUERIES), wide),
-            dma((6, PEERS)),
-            dma((6, PEERS)),
+            dma((6, LINE)),
+            dma((6, BLOCKS)),
             dma((2,)),
             dma((2,)),
-            dma((2, PEERS)),
-            dma((2, PEERS)),
+            dma((2, BLOCKS)),
+            dma((2, LINE)),
             dma((2, STEPS)),
             dma((2, STEPS)),
-            dma((2, PEERS)),
-            dma((2, PEERS)),
+            dma((2, BLOCKS)),
+            dma((2, LINE)),
         ],
         compiler_params=pltpu.CompilerParams(collective_id=0, has_side_effects=True),
         name="attention_backward",

time: 113 us -> 82 us (0.73)
  Pallas kernels: 109 us -> 77.5 us
    pallas_call x1, Pallas kernels: 109 us -> 77.5 us  [on_device(): pl.pallas_call(kernel, out_shape=(jax.ShapeDtypeStruct(query_rows.shape,...]
where the time goes in v2:
time: 82 us; the launch traced here: 81.8 us
  Pallas kernels  77.5 us (95%)
  local copies, waits for them, and re-layouts  3.67 us (4%)
    pallas_call x1, Pallas kernels, on_device(): pl.pallas_call(kernel, out_shape=(jax.ShapeDtypeStruct(query_rows.shape,...  77.5 us
    unnamed x7, local copies, waits for them, and re-layouts  3.67 us

profile of v2, /device:TPU:1, one launch (start us, length us, event | category | flops | bytes accessed | tf_op | source)
XLA Modules:
  0.0 81.8 jit_solution(9521214544998361515)
XLA Ops:
  0.6 77.5 %attention_backward.1 = (bf16[128,2048]{1,0:T(8,128)(2,1)}, bf16[128,1024]{1,0:T(8,128)(2,1)}, bf16[128,1024]{1,0:T(8,128)(2,1)}) custom-call(bf16[128,2048]{1,0:T(8,128)(2,1)} %query_in.1, bf16[128,1024]{1,0:T(8,128)(2,1)} %key_in.1, bf16[128,1024]{1,0:T(8,128)(2,1)} %value_in.1, bf16[128,2048]{1,0:T(8,128)(2,1)} %grad_in.1), custom_call_target="tpu_custom_call" | custom-call | tf_op jit(solution)/shard_map/attention_backward/pallas_call | solution.py:374
  78.1 0.0 copy-start.1
  78.1 1.9 %copy.10 = bf16[128,2048]{1,0:T(8,128)(2,1)} copy(bf16[128,2048]{1,0:T(8,128)(2,1)} %get-tuple-element.6) | data formatting | bytes 1048576
  80.1 0.0 copy-done.1
  80.1 0.0 copy-start
  80.1 0.7 copy.11
  80.8 0.3 copy-done
  81.1 0.7 copy.12
Async XLA Ops:
  78.1 1.9 %copy-start.1 = (bf16[128,1024]{1,0:T(8,128)(2,1)S(1)}, bf16[128,1024]{1,0:T(8,128)(2,1)}, u32[]{:S(2)}) copy-start(bf16[128,1024]{1,0:T(8,128)(2,1)} %get-tuple-element.7) | copy-start | bytes 786436
  80.1 1.0 %copy-start = (bf16[128,1024]{1,0:T(8,128)(2,1)S(1)}, bf16[128,1024]{1,0:T(8,128)(2,1)}, u32[]{:S(2)}) copy-start(bf16[128,1024]{1,0:T(8,128)(2,1)} %get-tuple-element.8) | copy-start | bytes 786436

commit v3 on v2

--- a/solution.py
+++ b/solution.py
@@ -57,6 +57,9 @@
     back_recv,
     own_send,
     own_recv,
+    answer_sem,
+    chain_sem,
+    seam_sem,
 ):
     seq = lax.axis_index("seq")
     head = lax.axis_index("head")
@@ -69,6 +72,8 @@
     alone = core == y_lo
     span = (x * 2 + core) * DEPTH + z
     span_count = lax.axis_size("seq") // 2
+    first, last = span == 0, span == span_count - 1
+    below, above = z > 0, z < DEPTH - 1
 
     def chip(other_y, other_core):
         other = (x * 2 + other_y % 2) * (2 * DEPTH) + z * 2 + other_core
@@ -142,14 +147,27 @@
         greet(device)
     for place in range(4):
         greet(chip(place * 2 + core, 1 - y_lo))
-    greet(following)
-    greet(preceding)
+
+    foot = (z == 0) & (core == 1) & (x < span_count // (2 * DEPTH) - 1)
 
     @pl.when(jnp.logical_not(alone))
     def _():
         greet(near_home[1])
 
-    pl.semaphore_wait(barrier, len(homes) + 6 + jnp.where(alone, 0, 1))
+    @pl.when(above)
+    def _():
+        greet(following)
+
+    @pl.when((z == 0) & (core == 0) & (x > 0))
+    def _():
+        greet(span_home(span - DEPTH))
+
+    heard = len(homes) + 4 + jnp.where(alone, 0, 1) + jnp.where(below | foot, 1, 0)
+    pl.semaphore_wait(barrier, heard)
+
+    @pl.when(below)
+    def _():
+        pl.semaphore_signal(answer_sem, inc=1, device_id=preceding, device_id_type=MESH)
 
     for kind in KINDS:
         for home, device in homes:
@@ -161,6 +179,31 @@
 
     key_sum[...] = jnp.zeros_like(key_sum)
     value_sum[...] = jnp.zeros_like(value_sum)
+
+    @pl.when(first)
+    def _():
+        keys[0:W, :] = jnp.zeros((W, HEAD_SIZE), jnp.bfloat16)
+        values[0:W, :] = jnp.zeros((W, HEAD_SIZE), jnp.bfloat16)
+
+    @pl.when(last)
+    def _():
+        back_landing[...] = jnp.zeros_like(back_landing)
+
+    @pl.when(above)
+    def _():
+        pl.semaphore_wait(answer_sem, 1)
+
+    @pl.when(below)
+    def _():
+        pl.semaphore_wait(chain_sem, 1)
+
+    @pl.when(above)
+    def _():
+        pl.semaphore_signal(chain_sem, inc=1, device_id=following, device_id_type=MESH)
+
+    @pl.when(jnp.logical_not(above | last))
+    def _():
+        pl.semaphore_signal(seam_sem, inc=1, device_id=following, device_id_type=MESH)
 
     def halo(which):
         array = keys if which == 0 else values
@@ -174,16 +217,28 @@
         )
 
     wait_in(K)
-    halo(0).start()
+    @pl.when(jnp.logical_not(last))
+    def _():
+        halo(0).start()
+
     wait_in(V)
-    halo(1).start()
-    halo(0).wait_recv()
+    @pl.when(jnp.logical_not(last))
+    def _():
+        halo(1).start()
+
+    @pl.when(jnp.logical_not(first))
+    def _():
+        halo(0).wait_recv()
+
 
     @pl.loop(0, 2 * W // CHUNK)
     def _(chunk):
         keys_t[chunk] = keys[rows(chunk, CHUNK), :].T
 
-    halo(1).wait_recv()
+    @pl.when(jnp.logical_not(first))
+    def _():
+        halo(1).wait_recv()
+
 
     key_row = lax.broadcasted_iota(jnp.int32, (CHUNK, QUERIES), 0)
     query_row = lax.broadcasted_iota(jnp.int32, (CHUNK, QUERIES), 1)
@@ -259,17 +314,25 @@
             device_id_type=MESH,
         )
 
-    def send_query(q_head):
-        for block, device in owners:
-            query_remote(q_head, block, device, y).start()
-
-        @pl.when(alone)
-        def _():
-            query_local(q_head).start()
-
-        @pl.when(jnp.logical_not(alone))
-        def _():
-            query_remote(q_head, *near_owner, y).start()
+    def send_rows(step, local, remote):
+        for block in (2 * step, 2 * step + 1):
+            device = chip(block % 4 * 2 + core, block // 4)
+            here = alone & (block == mine)
+
+            @pl.when(here)
+            def _():
+                local()
+
+            @pl.when(jnp.logical_not(here))
+            def _():
+                remote(block, device)
+
+    def send_query(q_head, step):
+        send_rows(
+            step,
+            lambda: query_local(q_head).start(),
+            lambda block, device: query_remote(q_head, block, device, y).start(),
+        )
 
     def back(which, step):
         return pltpu.make_async_remote_copy(
@@ -287,10 +350,14 @@
     @pl.loop(0, STEPS)
     def _(step):
         compute(0, step)
+        send_query(0, step)
 
     wait_in(Q1)
     wait_in(G1)
-    send_query(0)
+
+    @pl.when(jnp.logical_not(below | first))
+    def _():
+        pl.semaphore_wait(seam_sem, 1)
 
     @pl.loop(0, STEPS)
     def _(step):
@@ -298,10 +365,13 @@
         at = rows(step, QUERIES)
         back_stage[0, at, :] = key_sum[at, :].astype(jnp.bfloat16)
         back_stage[1, at, :] = value_sum[at, :].astype(jnp.bfloat16)
-        back(0, step).start()
-        back(1, step).start()
-
-    send_query(1)
+
+        @pl.when(jnp.logical_not(first))
+        def _():
+            back(0, step).start()
+            back(1, step).start()
+
+        send_query(1, step)
 
     def own_out(which):
         return key_out if which == 0 else value_out
@@ -327,25 +397,29 @@
     def _(step):
         at = rows(step, QUERIES)
         own = rows(STEPS + step, QUERIES)
+
+        @pl.when(jnp.logical_not(last))
+        def _():
+            back(0, step).wait_recv()
+            back(1, step).wait_recv()
+
         for which, sums in ((0, key_sum), (1, value_sum)):
-            back(which, step).wait_recv()
             own_stage[which, at, :] = (
                 sums[own, :] + back_landing[which, at, :].astype(jnp.float32)
             ).astype(jnp.bfloat16)
 
-    for which in (0, 1):
-        for block, device in owners:
-            own_remote(which, block, device, y).start()
-
-    @pl.when(alone)
-    def _():
-        for which in (0, 1):
-            own_local(which).start()
+        def local():
+            own_local(0).start()
+            own_local(1).start()
+
+        def remote(block, device):
+            own_remote(0, block, device, y).start()
+            own_remote(1, block, device, y).start()
+
+        send_rows(step, local, remote)
 
     @pl.when(jnp.logical_not(alone))
     def _():
-        for which in (0, 1):
-            own_remote(which, *near_owner, y).start()
         for kind in KINDS:
             remote_in(kind, *near_home, mine).wait_send()
         for which in (0, 1):
@@ -355,10 +429,18 @@
     for kind in KINDS:
         for home, device in homes:
             remote_in(kind, home, device, mine).wait_send()
+    @pl.when(jnp.logical_not(last))
+    def _():
+        halo(0).wait_send()
+        halo(1).wait_send()
+
+    @pl.when(jnp.logical_not(first))
+    def _():
+        for step in range(STEPS):
+            back(0, step).wait_send()
+            back(1, step).wait_send()
+
     for which in (0, 1):
-        halo(which).wait_send()
-        for step in range(STEPS):
-            back(which, step).wait_send()
         for block, device in owners:
             query_remote(which, block, device, y).wait_send()
             own_remote(which, block, device, y).wait_send()
@@ -367,18 +449,31 @@
             own_remote(which, mine, device, home).wait_recv()
 
 
+def store(query_from, key_from, value_from, query_to, key_to, value_to, done):
+    pairs = ((query_from, query_to), (key_from, key_to), (value_from, value_to))
+    copies = [
+        pltpu.make_async_copy(source, target, done.at[index])
+        for index, (source, target) in enumerate(pairs)
+    ]
+    for copy in copies:
+        copy.start()
+    for copy in copies:
+        copy.wait()
+
+
 def on_device(query_rows, key_rows, saved_value_rows, out_grad):
     dma = pltpu.SemaphoreType.DMA
     low, wide = jnp.bfloat16, jnp.float32
     anywhere = pl.BlockSpec(memory_space=pl.ANY)
-    return pl.pallas_call(
+    in_hbm = pl.BlockSpec(memory_space=pltpu.HBM)
+    results = pl.pallas_call(
         kernel,
         out_shape=(
-            jax.ShapeDtypeStruct(query_rows.shape, low),
-            jax.ShapeDtypeStruct(key_rows.shape, low),
-            jax.ShapeDtypeStruct(saved_value_rows.shape, low),
+            pltpu.VMEM(query_rows.shape, low),
+            pltpu.VMEM(key_rows.shape, low),
+            pltpu.VMEM(saved_value_rows.shape, low),
         ),
-        in_specs=[anywhere] * 4,
+        in_specs=[in_hbm] * 4,
         out_specs=(anywhere,) * 3,
         scratch_shapes=[
             pltpu.VMEM((2 * W, HEAD_SIZE), low),
@@ -404,10 +499,25 @@
             dma((2, STEPS)),
             dma((2, BLOCKS)),
             dma((2, LINE)),
+            pltpu.SemaphoreType.REGULAR,
+            pltpu.SemaphoreType.REGULAR,
+            pltpu.SemaphoreType.REGULAR,
         ],
-        compiler_params=pltpu.CompilerParams(collective_id=0, has_side_effects=True),
+        compiler_params=pltpu.CompilerParams(
+            collective_id=0, has_side_effects=True
+        ),
         name="attention_backward",
     )(query_rows, key_rows, saved_value_rows, out_grad)
+    in_vmem = pl.BlockSpec(memory_space=pltpu.VMEM)
+    return pl.pallas_call(
+        store,
+        out_shape=tuple(jax.ShapeDtypeStruct(result.shape, low) for result in results),
+        in_specs=[in_vmem] * 3,
+        out_specs=(in_hbm,) * 3,
+        scratch_shapes=[dma((3,))],
+        compiler_params=pltpu.CompilerParams(vmem_limit_bytes=4 * 2**20),
+        name="store",
+    )(*results)
 
 
 def solution(mesh):

time: 82 us -> 71.1 us (0.87)
  Pallas kernels: 77.5 us -> 70.3 us
  local copies, waits for them, and re-layouts: 3.67 us -> 0 us
    pallas_call x1 -> x2, Pallas kernels: 77.5 us -> 70.3 us  [the longest x1 69.3 us: on_device(): pl.pallas_call(kernel, out_shape=(pltpu.VMEM(query_rows.shape, low), pltp...]
    unnamed x7 -> x0, local copies, waits for them, and re-layouts: 3.67 us -> none
where the time goes in v3:
time: 71.1 us; the launch traced here: 70.9 us
  Pallas kernels  70.3 us (99%)
    pallas_call x1, Pallas kernels, on_device(): pl.pallas_call(kernel, out_shape=(pltpu.VMEM(query_rows.shape, low), pltp...  69.3 us

profile of v3, /device:TPU:1, one launch (start us, length us, event | category | flops | bytes accessed | tf_op | source)
XLA Modules:
  0.0 70.9 jit_solution(11646414728158612804)
XLA Ops:
  0.6 69.3 %attention_backward.1 = (bf16[128,2048]{1,0:T(8,128)(2,1)S(1)}, bf16[128,1024]{1,0:T(8,128)(2,1)S(1)}, bf16[128,1024]{1,0:T(8,128)(2,1)S(1)}) custom-call(bf16[128,2048]{1,0:T(8,128)(2,1)} %query_in.1, bf16[128,1024]{1,0:T(8,128)(2,1)} %key_in.1, bf16[128,1024]{1,0:T(8,128)(2,1)} %value_in.1, bf16[128,2048]{1,0:T(8,128)(2,1)} %grad_in.1), custom_call_target="tpu_custom_call" | custom-call | tf_op jit(solution)/shard_map/attention_backward/pallas_call | solution.py:469
  69.9 1.0 %store.1 = (bf16[128,2048]{1,0:T(8,128)(2,1)}, bf16[128,1024]{1,0:T(8,128)(2,1)}, bf16[128,1024]{1,0:T(8,128)(2,1)}) custom-call(bf16[128,2048]{1,0:T(8,128)(2,1)S(1)} %get-tuple-element.6.query_from, bf16[128,1024]{1,0:T(8,128)(2,1)S(1)} %get-tuple-element.7.key_from, bf16[128,1024]{1,0:T(8,128)(2,1)S(1)} %get-tuple-element.8.value_from), custom_call_target="tpu_custom_call" | custom-call | tf_op jit(solution)/shard_map/store/pallas_call | solution.py:512

commit v4 on v3

--- a/solution.py
+++ b/solution.py
@@ -21,7 +21,7 @@
 masked_value = -1e30
 contract_last = (((1,), (1,)), ((), ()))
 
-HOMES = (1, 7, 2, 6, 3, 5, 4)
+HOMES = (3, 5, 1, 7, 4, 2, 6)
 OWNERS = ((0, 1), (1, 1), (0, 3), (1, 3), (0, 2), (1, 2), (1, 0))
 KINDS = K, V, Q0, G0, Q1, G1 = range(6)
 
@@ -60,6 +60,7 @@
     answer_sem,
     chain_sem,
     seam_sem,
+    foot_sem,
 ):
     seq = lax.axis_index("seq")
     head = lax.axis_index("head")
@@ -149,6 +150,7 @@
         greet(chip(place * 2 + core, 1 - y_lo))
 
     foot = (z == 0) & (core == 1) & (x < span_count // (2 * DEPTH) - 1)
+    next_foot = (z == 0) & (core == 0) & (x > 0)
 
     @pl.when(jnp.logical_not(alone))
     def _():
@@ -158,16 +160,21 @@
     def _():
         greet(following)
 
-    @pl.when((z == 0) & (core == 0) & (x > 0))
-    def _():
-        greet(span_home(span - DEPTH))
-
-    heard = len(homes) + 4 + jnp.where(alone, 0, 1) + jnp.where(below | foot, 1, 0)
+    @pl.when(foot)
+    def _():
+        greet(span_home(span + DEPTH))
+
+    heard = len(homes) + 4 + jnp.where(alone, 0, 1) + jnp.where(below | next_foot, 1, 0)
     pl.semaphore_wait(barrier, heard)
 
     @pl.when(below)
     def _():
         pl.semaphore_signal(answer_sem, inc=1, device_id=preceding, device_id_type=MESH)
+
+    @pl.when(next_foot)
+    def _():
+        device = span_home(span - DEPTH)
+        pl.semaphore_signal(foot_sem, inc=1, device_id=device, device_id_type=MESH)
 
     for kind in KINDS:
         for home, device in homes:
@@ -196,6 +203,10 @@
     @pl.when(below)
     def _():
         pl.semaphore_wait(chain_sem, 1)
+
+    @pl.when(foot)
+    def _():
+        pl.semaphore_wait(foot_sem, 1)
 
     @pl.when(above)
     def _():
@@ -350,10 +361,15 @@
     @pl.loop(0, STEPS)
     def _(step):
         compute(0, step)
-        send_query(0, step)
+
+        @pl.when(step < 2)
+        def _():
+            send_query(0, step)
 
     wait_in(Q1)
     wait_in(G1)
+    for step in (2, 3):
+        send_query(0, step)
 
     @pl.when(jnp.logical_not(below | first))
     def _():
@@ -502,6 +518,7 @@
             pltpu.SemaphoreType.REGULAR,
             pltpu.SemaphoreType.REGULAR,
             pltpu.SemaphoreType.REGULAR,
+            pltpu.SemaphoreType.REGULAR,
         ],
         compiler_params=pltpu.CompilerParams(
             collective_id=0, has_side_effects=True

time: 71.1 us -> 69.4 us (0.976)
  Pallas kernels: 70.3 us -> 68.7 us
    pallas_call x1, Pallas kernels: 69.3 us -> 67.7 us  [on_device(): pl.pallas_call(kernel, out_shape=(pltpu.VMEM(query_rows.shape, low), pltp...]
where the time goes in v4:
time: 69.4 us; the launch traced here: 69.3 us
  Pallas kernels  68.7 us (99%)
    pallas_call x1, Pallas kernels, on_device(): pl.pallas_call(kernel, out_shape=(pltpu.VMEM(query_rows.shape, low), pltp...  67.7 us

profile of v4, /device:TPU:1, one launch (start us, length us, event | category | flops | bytes accessed | tf_op | source)
XLA Modules:
  0.0 69.3 jit_solution(17268313683397232166)
XLA Ops:
  0.6 67.7 %attention_backward.1 = (bf16[128,2048]{1,0:T(8,128)(2,1)S(1)}, bf16[128,1024]{1,0:T(8,128)(2,1)S(1)}, bf16[128,1024]{1,0:T(8,128)(2,1)S(1)}) custom-call(bf16[128,2048]{1,0:T(8,128)(2,1)} %query_in.1, bf16[128,1024]{1,0:T(8,128)(2,1)} %key_in.1, bf16[128,1024]{1,0:T(8,128)(2,1)} %value_in.1, bf16[128,2048]{1,0:T(8,128)(2,1)} %grad_in.1), custom_call_target="tpu_custom_call" | custom-call | tf_op jit(solution)/shard_map/attention_backward/pallas_call | solution.py:485
  68.3 1.0 %store.1 = (bf16[128,2048]{1,0:T(8,128)(2,1)}, bf16[128,1024]{1,0:T(8,128)(2,1)}, bf16[128,1024]{1,0:T(8,128)(2,1)}) custom-call(bf16[128,2048]{1,0:T(8,128)(2,1)S(1)} %get-tuple-element.6.query_from, bf16[128,1024]{1,0:T(8,128)(2,1)S(1)} %get-tuple-element.7.key_from, bf16[128,1024]{1,0:T(8,128)(2,1)S(1)} %get-tuple-element.8.value_from), custom_call_target="tpu_custom_call" | custom-call | tf_op jit(solution)/shard_map/store/pallas_call | solution.py:529

commit v5 on v4

--- a/solution.py
+++ b/solution.py
@@ -1,3 +1,5 @@
+import math
+
 import jax
 import jax.numpy as jnp
 from jax import lax
@@ -18,10 +20,11 @@
 MESH = pl.DeviceIdType.MESH
 
 score_scale = 168.0 ** (-0.5)
+binary_scale = score_scale * math.log2(math.e)
 masked_value = -1e30
 contract_last = (((1,), (1,)), ((), ()))
 
-HOMES = (3, 5, 1, 7, 4, 2, 6)
+HOMES = (3, 5, 4, 1, 7, 2, 6)
 OWNERS = ((0, 1), (1, 1), (0, 3), (1, 3), (0, 2), (1, 2), (1, 0))
 KINDS = K, V, Q0, G0, Q1, G1 = range(6)
 
@@ -266,7 +269,7 @@
                     contract_last,
                     preferred_element_type=jnp.float32,
                 )
-                * score_scale
+                * binary_scale
             )
             if part < CHUNKS - 1:
                 absent = (span == 0) & (step + part < W // CHUNK)
@@ -281,7 +284,7 @@
         total = jnp.zeros((1, QUERIES), jnp.float32)
         delta = jnp.zeros((1, QUERIES), jnp.float32)
         for part in range(CHUNKS):
-            weights = jnp.exp(score_buf[part] - peak)
+            weights = jnp.exp2(score_buf[part] - peak)
             prob_grad = lax.dot_general(
                 values[rows(step + part, CHUNK), :],
                 grad,
@@ -297,7 +300,7 @@
         query_grad = jnp.zeros((HEAD_SIZE, QUERIES), jnp.float32)
         for part in range(CHUNKS):
             attention = score_buf[part] * inverse
-            score_grad = (score_scale * attention * (prob_buf[part] - delta)).astype(jnp.bfloat16)
+            score_grad = (attention * (prob_buf[part] - delta)).astype(jnp.bfloat16)
             at = rows(step + part, CHUNK)
             value_sum[at, :] += jnp.dot(
                 attention.astype(jnp.bfloat16), grad, preferred_element_type=jnp.float32
@@ -306,7 +309,7 @@
             query_grad = query_grad + jnp.dot(
                 keys_t[step + part], score_grad, preferred_element_type=jnp.float32
             )
-        query_stage[q_head, rows(step, QUERIES), :] = query_grad.T.astype(jnp.bfloat16)
+        query_stage[q_head, rows(step, QUERIES), :] = (score_scale * query_grad.T).astype(jnp.bfloat16)
 
     def query_local(q_head):
         return pltpu.make_async_copy(
@@ -379,7 +382,7 @@
     def _(step):
         compute(1, step)
         at = rows(step, QUERIES)
-        back_stage[0, at, :] = key_sum[at, :].astype(jnp.bfloat16)
+        back_stage[0, at, :] = (score_scale * key_sum[at, :]).astype(jnp.bfloat16)
         back_stage[1, at, :] = value_sum[at, :].astype(jnp.bfloat16)
 
         @pl.when(jnp.logical_not(first))
@@ -410,7 +413,8 @@
         )
 
     @pl.loop(0, STEPS)
-    def _(step):
+    def _(turn):
+        step = jnp.where(y < LINE // 2, turn + 1 - 2 * (turn % 2), turn)
         at = rows(step, QUERIES)
         own = rows(STEPS + step, QUERIES)
 
@@ -419,9 +423,9 @@
             back(0, step).wait_recv()
             back(1, step).wait_recv()
 
-        for which, sums in ((0, key_sum), (1, value_sum)):
+        for which, sums, scale in ((0, key_sum, score_scale), (1, value_sum, 1.0)):
             own_stage[which, at, :] = (
-                sums[own, :] + back_landing[which, at, :].astype(jnp.float32)
+                scale * sums[own, :] + back_landing[which, at, :].astype(jnp.float32)
             ).astype(jnp.bfloat16)
 
         def local():

time: 69.4 us -> 70.2 us (1.012)
    pallas_call x1, Pallas kernels: 67.7 us -> 68.4 us  [on_device(): pl.pallas_call(kernel, out_shape=(pltpu.VMEM(query_rows.shape, low), pltp...]
where the time goes in v5:
time: 70.2 us; the launch traced here: 70.1 us
  Pallas kernels  69.4 us (99%)
    pallas_call x1, Pallas kernels, on_device(): pl.pallas_call(kernel, out_shape=(pltpu.VMEM(query_rows.shape, low), pltp...  68.4 us

profile of v5, /device:TPU:1, one launch (start us, length us, event | category | flops | bytes accessed | tf_op | source)
XLA Modules:
  0.0 70.1 jit_solution(3957344018054056769)
XLA Ops:
  0.6 68.4 %attention_backward.1 = (bf16[128,2048]{1,0:T(8,128)(2,1)S(1)}, bf16[128,1024]{1,0:T(8,128)(2,1)S(1)}, bf16[128,1024]{1,0:T(8,128)(2,1)S(1)}) custom-call(bf16[128,2048]{1,0:T(8,128)(2,1)} %query_in.1, bf16[128,1024]{1,0:T(8,128)(2,1)} %key_in.1, bf16[128,1024]{1,0:T(8,128)(2,1)} %value_in.1, bf16[128,2048]{1,0:T(8,128)(2,1)} %grad_in.1), custom_call_target="tpu_custom_call" | custom-call | tf_op jit(solution)/shard_map/attention_backward/pallas_call | solution.py:489
  69.1 1.0 %store.1 = (bf16[128,2048]{1,0:T(8,128)(2,1)}, bf16[128,1024]{1,0:T(8,128)(2,1)}, bf16[128,1024]{1,0:T(8,128)(2,1)}) custom-call(bf16[128,2048]{1,0:T(8,128)(2,1)S(1)} %get-tuple-element.6.query_from, bf16[128,1024]{1,0:T(8,128)(2,1)S(1)} %get-tuple-element.7.key_from, bf16[128,1024]{1,0:T(8,128)(2,1)S(1)} %get-tuple-element.8.value_from), custom_call_target="tpu_custom_call" | custom-call | tf_op jit(solution)/shard_map/store/pallas_call | solution.py:533
